TPU v7x, 32 devices: a whole 2x2x4 slice. The times are simulated.
32 devices in a mesh: prow: 4 (over y, x), pcol: 8 (over z, core).
Axes of the slice: x: 2, y: 2, z: 4, core: 2. Of those that a mesh axis runs over, the one named last changes fastest.
Arguments:
- ancestor: float32 [12288, 12288], P('prow', 'pcol'), may hold values from -448 to 15360, as said below
- factor: bfloat16 [2, 12288, 256], P(None, 'prow'), may hold values from -0.0009765625 to 0.0009765625
- inverse_diag: bfloat16 [2, 256, 256], replicated, may hold values from -6 to 6
- block_mask: int32 [2, 48], replicated, may hold values 0 or 1
Outputs:
- column_block: float32 [2, 12288, 256], P(None, ('prow', 'pcol'))
- diagonal: float32 [2, 256, 256], replicated
Inputs may be any that keep to these rules, and one draw needn't show every extreme that they name: `ancestor`: symmetric.
All inputs are finite; a program needn't handle non-finite values.
Results may differ from a plain program's by a relative error of at most 0.0003.
Values may be sent and summed in bfloat16 or wider, within the bound.
A program may use at most 64 MiB of HBM per device.

v0:
```python
import jax
import jax.numpy as jnp
from jax import lax
from jax.sharding import PartitionSpec as P

WIDTH = 256


def broadcast(shard, axis, root):
    mine = lax.axis_index(axis) == root
    return lax.psum(jnp.where(mine, shard, jnp.zeros_like(shard)), axis)


def multiply(ancestor, received, col_mask, own_mask):
    weighted = received.astype(jnp.float32) * col_mask[:, :, None]
    product = jnp.einsum(
        "ij,kjw->kiw",
        ancestor,
        weighted,
        precision=lax.Precision.HIGHEST,
        preferred_element_type=jnp.float32,
    )
    return -own_mask[:, :, None] * product


def reduced_term(own_rows, column_block, column):
    slab = column_block.shape[1]
    own_slab = lax.dynamic_slice_in_dim(own_rows, column * slab, slab, 1)
    return jnp.einsum(
        "kiw,kiv->kwv",
        own_slab,
        column_block,
        precision=lax.Precision.HIGHEST,
        preferred_element_type=jnp.float32,
    )


def shards(ancestor, factor, inverse_diag, block_mask):
    rows_here = ancestor.shape[0]
    cols_here = ancestor.shape[1]
    n_rows = lax.axis_size("prow")
    n_cols = lax.axis_size("pcol")
    per_row = n_cols // n_rows
    column = lax.axis_index("pcol")
    grid_row = lax.axis_index("prow")
    root_row = column // per_row
    offset = column % per_row * cols_here
    row_mask = jnp.repeat(block_mask, WIDTH, axis=1).astype(jnp.float32)
    own_mask = lax.dynamic_slice_in_dim(row_mask, grid_row * rows_here, rows_here, 1)
    col_mask = lax.dynamic_slice_in_dim(row_mask, column * cols_here, cols_here, 1)
    own_rows = factor.astype(jnp.float32) * own_mask[:, :, None]
    col_part = lax.dynamic_slice_in_dim(factor, offset, cols_here, 1)
    pieces = []
    blocks = []
    for supernode in range(factor.shape[0]):
        received = broadcast(col_part[supernode : supernode + 1], "prow", root_row)
        negated_one = multiply(
            ancestor,
            received,
            col_mask[supernode : supernode + 1],
            own_mask[supernode : supernode + 1],
        )
        blocks.append(lax.psum_scatter(negated_one, "pcol", scatter_dimension=1, tiled=True))
        pieces.append(negated_one)
    column_block = jnp.concatenate(blocks, 0)
    term = reduced_term(own_rows, column_block, column)
    total = lax.psum(term, ("prow", "pcol"))
    diagonal = inverse_diag.astype(jnp.float32) - total
    return (column_block, diagonal)


def solution(mesh):
    return jax.shard_map(
        shards,
        mesh=mesh,
        in_specs=(P("prow", "pcol"), P(None, "prow", None), P(), P()),
        out_specs=(P(None, ("prow", "pcol"), None), P()),
        check_vma=False,
    )
```

profile of v0, /device:TPU:0, one launch (start us, length us, event | category | flops | bytes accessed | tf_op | source)
XLA Modules:
  0.0 335.2 jit_solution(11929056268012232022)
XLA Ops:
  7.2 0.0 copy-start.2
  7.2 0.0 all-reduce.6.cloned.1.call-start
  7.2 2.8 dynamic-slice_select_fusion
  10.1 0.0 all-reduce.6.cloned.1.call-update
  10.1 0.0 reduce-scatter.3.cloned.1.call-start
  10.1 0.0 copy-done.2
  10.2 0.1 broadcast_bitcast_fusion
  10.2 0.1 copy.11
  10.3 0.1 dynamic-slice_reduce_fusion
  10.4 0.1 dynamic-slice_negate_fusion
  10.5 64.6 %all-reduce.6.cloned.1.call-done = (bf16[1,1536,256]{2,1,0:T(8,128)(2,1)}, bf16[1,1536,256]{2,1,0:T(8,128)(2,1)}) async-done(((bf16[1,1536,256]{2,1,0:T(8,128)(2,1)}, bf16[1,1536,256]{2,1,0:T(8,128)(2,1)}), (bf16[1,1536,256]{2,1,0:T(8,128)(2,1)}, bf16[1,1536,256]{2,1,0:T(8,128)(2,1)})) %all-reduce.6.cloned.1.call-update) | async-done | bytes 1572880 | tf_op jit(solution)/shard_map/psum | solution.py:11
  75.2 35.3 %fusion.3 = f32[1,3072,256]{1,2,0:T(8,128)} fusion(f32[3072,1536]{1,0:T(8,128)} %param.4, bf16[1,1536,256]{2,1,0:T(8,128)(2,1)} %get-tuple-element.6, f32[3072]{0:T(1024)S(1)} %bitcast.34, f32[1536]{0:T(1024)S(1)} %get-tuple-element.5), kind=kOutput, calls=%fused_computation.5 | convolution fusion | flops 14497087488 | bytes 22824960 | tf_op jit(solution)/shard_map/ij,kjw->kiw/dot_general | solution.py:16
  110.4 0.0 copy-start
  110.4 0.0 reduce-scatter.3.cloned.1.call-update
  110.4 0.2 reduce-scatter.5.cloned.1.call-start
  110.7 0.9 copy-done
  111.5 35.1 %fusion.1 = f32[1,3072,256]{1,2,0:T(8,128)} fusion(f32[3072,1536]{1,0:T(8,128)} %param.4, bf16[1,1536,256]{2,1,0:T(8,128)(2,1)S(1)} %copy-done, f32[3072]{0:T(1024)S(1)} %bitcast.33, f32[1536]{0:T(1024)S(1)} %get-tuple-element.4), kind=kOutput, calls=%fused_computation.2 | convolution fusion | flops 14497087488 | bytes 22824960 | tf_op jit(solution)/shard_map/ij,kjw->kiw/dot_general | solution.py:16
  146.7 0.0 reduce-scatter.5.cloned.1.call-update
  146.7 0.0 all-reduce.4.cloned.1.call-start
  146.7 1.0 constant_dynamic-slice_fusion.1
  147.8 0.0 copy-start.1
  147.8 0.2 copy.10
  148.0 2.9 reduce-scatter.3.cloned.1.call-done
  151.0 1.0 constant_dynamic-update-slice_fusion.1
  152.0 40.8 %reduce-scatter.5.cloned.1.call-done = f32[1,384,256]{1,2,0:T(8,128)} async-done(((f32[1,3072,256]{1,2,0:T(8,128)}), f32[1,384,256]{1,2,0:T(8,128)}) %reduce-scatter.5.cloned.1.call-update) | async-done | bytes 393232 | tf_op jit(solution)/shard_map/reduce_scatter | solution.py:63
  192.8 1.0 constant_dynamic-update-slice_fusion
  193.9 1.9 fusion.10
  195.8 0.0 all-reduce.4.cloned.1.call-update
  195.8 1.1 copy.8
  197.0 129.8 %all-reduce.4.cloned.1.call-done = f32[2,256,256]{2,1,0:T(8,128)} async-done(((f32[2,256,256]{2,1,0:T(8,128)}), f32[2,256,256]{2,1,0:T(8,128)}) %all-reduce.4.cloned.1.call-update) | async-done | bytes 524304 | tf_op jit(solution)/shard_map/psum | solution.py:67
  326.8 0.0 copy-done.1
  326.8 1.9 convert_subtract_fusion
  (3 shorter events, 0.0 us)
Async XLA Ops:
  7.2 3.0 copy-start.2
  7.2 68.0 %all-reduce.6.cloned.1.call-start = ((), (), s32[]{:S(2)}) async-start(), calls=%async_computation.5 | async-start | bytes 3145728 | tf_op jit(solution)/shard_map/psum | solution.py:11
  10.1 140.9 %reduce-scatter.3.cloned.1.call-start = ((), (), s32[]{:S(2)}) async-start(), calls=%async_computation.2 | async-start | bytes 3538944 | tf_op jit(solution)/shard_map/reduce_scatter | solution.py:63
  110.4 1.1 copy-start
  110.4 82.4 %reduce-scatter.5.cloned.1.call-start = ((), (), s32[]{:S(2)}) async-start(), calls=%async_computation.3 | async-start | bytes 3538944 | tf_op jit(solution)/shard_map/reduce_scatter | solution.py:63
  146.7 180.1 %all-reduce.4.cloned.1.call-start = ((), (), s32[]{:S(2)}) async-start(), calls=%async_computation.4 | async-start | bytes 1048576 | tf_op jit(solution)/shard_map/psum | solution.py:67
  147.8 179.0 %copy-start.1 = (bf16[2,256,256]{2,1,0:T(8,128)(2,1)S(1)}, bf16[2,256,256]{2,1,0:T(8,128)(2,1)}, u32[]{:S(2)}) copy-start(bf16[2,256,256]{2,1,0:T(8,128)(2,1)} %param.6) | copy-start | bytes 786436
Sparse Core Ops, SparseCore 0:
  11.7 63.4 all-reduce.5
  110.6 40.3 reduce-scatter.2
  153.3 39.5 reduce-scatter.4
  198.5 128.1 all-reduce.3
where the time goes:
time: 336 us; the launch traced here: 335 us
  waiting for transfers between devices  238 us (71%)
  matrix products  72.3 us (22%)
  between operations  13.9 us (4%)
  local copies, waits for them, and re-layouts  5.6 us (2%)
  other arithmetic  4.8 us (1%)
    psum x1, waiting for transfers between devices, shards(): total = lax.psum(term, ('prow', 'pcol'))  130 us
    dot_general x2, matrix products, multiply(): jnp.einsum('ij,kjw->kiw', ancestor, weighted, precision=lax.Precision.HIG...  70.4 us
    psum x1, waiting for transfers between devices, broadcast(): return lax.psum(jnp.where(mine, shard, jnp.zeros_like(shard)), axis)  64.6 us
    reduce_scatter x2, waiting for transfers between devices, shards(): lax.psum_scatter(negated_one, 'pcol', scatter_dimension=1, tiled=True)  43.8 us
  transfers between devices with their start and end apart: 4, of which 4 were waited for; matrix products, arithmetic and copies ran while one was open for 12% of the time, Pallas kernels for 0%

commit v1 on v0

--- a/solution.py
+++ b/solution.py
@@ -64,7 +64,7 @@
         pieces.append(negated_one)
     column_block = jnp.concatenate(blocks, 0)
     term = reduced_term(own_rows, column_block, column)
-    total = lax.psum(term, ("prow", "pcol"))
+    total = jnp.sum(lax.all_gather(term, ("prow", "pcol")), axis=0)
     diagonal = inverse_diag.astype(jnp.float32) - total
     return (column_block, diagonal)
 

time: 336 us -> 324 us (0.964)
  waiting for transfers between devices: 238 us -> 221 us
  other arithmetic: 4.8 us -> 10.7 us
    psum x1 -> x0, waiting for transfers between devices: 130 us -> none  [shards(): total = lax.psum(term, ('prow', 'pcol'))]
    all_gather x0 -> x1, waiting for transfers between devices: none -> 113 us  [shards(): total = jnp.sum(lax.all_gather(term, ('prow', 'pcol')), axis=0)]
    reduce_sum x0 -> x1, other arithmetic: none -> 6.93 us  [shards(): total = jnp.sum(lax.all_gather(term, ('prow', 'pcol')), axis=0)]
where the time goes in v1:
time: 324 us
  waiting for transfers between devices  221 us (68%)
  matrix products  72.3 us (22%)
  between operations  13.9 us (4%)
  other arithmetic  10.7 us (3%)
  local copies, waits for them, and re-layouts  5.6 us (2%)
    all_gather x1, waiting for transfers between devices, shards(): total = jnp.sum(lax.all_gather(term, ('prow', 'pcol')), axis=0)  113 us
    dot_general x2, matrix products, multiply(): jnp.einsum('ij,kjw->kiw', ancestor, weighted, precision=lax.Precision.HIG...  70.4 us
    psum x1, waiting for transfers between devices, broadcast(): return lax.psum(jnp.where(mine, shard, jnp.zeros_like(shard)), axis)  64.6 us
    reduce_scatter x2, waiting for transfers between devices, shards(): lax.psum_scatter(negated_one, 'pcol', scatter_dimension=1, tiled=True)  43.6 us
    reduce_sum x1, other arithmetic, shards(): total = jnp.sum(lax.all_gather(term, ('prow', 'pcol')), axis=0)  6.93 us
  transfers between devices with their start and end apart: 4, of which 4 were waited for; matrix products, arithmetic and copies ran while one was open for 12% of the time, Pallas kernels for 0%

profile of v1, /device:TPU:0, one launch (start us, length us, event | category | flops | bytes accessed | tf_op | source)
XLA Modules:
  0.0 324.2 jit_solution(7329764280495390541)
XLA Ops:
  7.2 0.0 copy-start.2
  7.2 0.0 all-reduce.3.cloned.1.call-start
  7.2 2.8 dynamic-slice_select_fusion
  10.1 0.0 all-reduce.3.cloned.1.call-update
  10.1 0.0 reduce-scatter.3.cloned.1.call-start
  10.1 0.0 copy-done.2
  10.2 0.1 broadcast_bitcast_fusion
  10.2 0.1 copy.14
  10.3 0.1 dynamic-slice_reduce_fusion
  10.4 0.1 dynamic-slice_negate_fusion
  10.5 64.6 %all-reduce.3.cloned.1.call-done = (bf16[1,1536,256]{2,1,0:T(8,128)(2,1)}, bf16[1,1536,256]{2,1,0:T(8,128)(2,1)}) async-done(((bf16[1,1536,256]{2,1,0:T(8,128)(2,1)}, bf16[1,1536,256]{2,1,0:T(8,128)(2,1)}), (bf16[1,1536,256]{2,1,0:T(8,128)(2,1)}, bf16[1,1536,256]{2,1,0:T(8,128)(2,1)})) %all-reduce.3.cloned.1.call-update) | async-done | bytes 1572880 | tf_op jit(solution)/shard_map/psum | solution.py:11
  75.2 35.3 %fusion.3 = f32[1,3072,256]{1,2,0:T(8,128)} fusion(f32[3072,1536]{1,0:T(8,128)} %param.4, bf16[1,1536,256]{2,1,0:T(8,128)(2,1)} %get-tuple-element.8, f32[3072]{0:T(1024)S(1)} %bitcast.36, f32[1536]{0:T(1024)S(1)} %get-tuple-element.7), kind=kOutput, calls=%fused_computation.5 | convolution fusion | flops 14497087488 | bytes 22824960 | tf_op jit(solution)/shard_map/ij,kjw->kiw/dot_general | solution.py:16
  110.4 0.0 copy-start
  110.4 0.0 reduce-scatter.3.cloned.1.call-update
  110.4 0.2 reduce-scatter.5.cloned.1.call-start
  110.7 0.9 copy-done
  111.5 35.1 %fusion.1 = f32[1,3072,256]{1,2,0:T(8,128)} fusion(f32[3072,1536]{1,0:T(8,128)} %param.4, bf16[1,1536,256]{2,1,0:T(8,128)(2,1)S(1)} %copy-done, f32[3072]{0:T(1024)S(1)} %bitcast.35, f32[1536]{0:T(1024)S(1)} %get-tuple-element.6), kind=kOutput, calls=%fused_computation.2 | convolution fusion | flops 14497087488 | bytes 22824960 | tf_op jit(solution)/shard_map/ij,kjw->kiw/dot_general | solution.py:16
  146.7 0.0 reduce-scatter.5.cloned.1.call-update
  146.7 0.3 all-gather.3.cloned.1.call-start
  147.0 1.0 constant_dynamic-slice_fusion.1
  148.0 0.2 copy.13
  148.2 2.7 reduce-scatter.3.cloned.1.call-done
  151.0 1.0 constant_dynamic-update-slice_fusion.1
  152.0 40.8 %reduce-scatter.5.cloned.1.call-done = f32[1,384,256]{1,2,0:T(8,128)} async-done(((f32[1,3072,256]{1,2,0:T(8,128)}), f32[1,384,256]{1,2,0:T(8,128)}) %reduce-scatter.5.cloned.1.call-update) | async-done | bytes 393232 | tf_op jit(solution)/shard_map/reduce_scatter | solution.py:63
  192.8 1.0 constant_dynamic-update-slice_fusion
  193.9 1.9 fusion.10
  195.8 0.0 all-gather.3.cloned.1.call-update
  195.8 1.1 copy.11
  197.0 112.9 %all-gather.3.cloned.1.call-done = f32[64,256,256]{2,1,0:T(8,128)} async-done(((f32[2,256,256]{2,1,0:T(8,128)}), f32[64,256,256]{2,1,0:T(8,128)}) %all-gather.3.cloned.1.call-update) | async-done | bytes 16777232 | tf_op jit(solution)/shard_map/all_gather | solution.py:67
  309.8 0.0 copy-start.1
  309.8 6.9 %reduce_sum.9 = f32[2,256,256]{2,1,0:T(8,128)S(1)} reduce(f32[32,2,256,256]{3,2,1,0:T(8,128)} %bitcast.31, f32[]{:T(128)} %constant.44.clone.1), dimensions={0}, to_apply=%region_4.5 | reduce | flops 4063232 | bytes 17301508 | tf_op jit(solution)/shard_map/reduce_sum | solution.py:67
  316.8 0.0 copy-done.1
  316.8 0.8 convert_subtract_fusion
  (3 shorter events, 0.0 us)
Async XLA Ops:
  7.2 3.0 copy-start.2
  7.2 68.0 %all-reduce.3.cloned.1.call-start = ((), (), s32[]{:S(2)}) async-start(), calls=%async_computation.5 | async-start | bytes 3145728 | tf_op jit(solution)/shard_map/psum | solution.py:11
  10.1 140.9 %reduce-scatter.3.cloned.1.call-start = ((), (), s32[]{:S(2)}) async-start(), calls=%async_computation.2 | async-start | bytes 3538944 | tf_op jit(solution)/shard_map/reduce_scatter | solution.py:63
  110.4 1.1 copy-start
  110.4 82.4 %reduce-scatter.5.cloned.1.call-start = ((), (), s32[]{:S(2)}) async-start(), calls=%async_computation.3 | async-start | bytes 3538944 | tf_op jit(solution)/shard_map/reduce_scatter | solution.py:63
  146.7 163.2 %all-gather.3.cloned.1.call-start = ((), (), s32[]{:S(2)}) async-start(), calls=%async_computation.4 | async-start | bytes 17301504 | tf_op jit(solution)/shard_map/all_gather | solution.py:67
  309.8 6.9 %copy-start.1 = (bf16[2,256,256]{2,1,0:T(8,128)(2,1)S(1)}, bf16[2,256,256]{2,1,0:T(8,128)(2,1)}, u32[]{:S(2)}) copy-start(bf16[2,256,256]{2,1,0:T(8,128)(2,1)} %param.6) | copy-start | bytes 786436
Sparse Core Ops, SparseCore 0:
  11.7 63.4 all-reduce.2
  110.6 40.3 reduce-scatter.2
  153.3 39.5 reduce-scatter.4
  196.3 113.5 all-gather.2
